TPU v7x, 256 devices: a whole 4x4x8 slice. The times are simulated.
256 devices in a mesh: pair: 8 (over x, y_lo), row: 32 (over y_hi, z, core).
Axes of the slice: x: 4, y: 4 (y_hi: 2, y_lo: 2; y = y_hi * 2 + y_lo), z: 8, core: 2. Of those that a mesh axis runs over, the one named last changes fastest.
Arguments:
- matrix: float32 [2, 131072, 1024], P(None, 'row', 'pair'), may hold values from -100 to 100, as said below
Outputs:
- rotated_matrix: float32 [2, 131072, 1024], P(None, 'row', 'pair')
Inputs may be any that keep to these rules, and one draw needn't show every extreme that they name: `matrix`: entries are real values with column blocks that are far from orthogonal to one another.
All inputs are finite; a program needn't handle non-finite values.
Results may differ from a plain program's by a relative error of at most 0.00014.
Values sent between devices are 32-bit elements; how exact they have to be, the bound alone decides.
A program may use at most 64 MiB of HBM per device.

v0:
```python
import jax
import jax.numpy as jnp
from jax import lax
from jax.sharding import PartitionSpec as P

STEPS = 2
SWEEPS = 2
NEWTON = 3


def shifted(block, axis, distance):
    devices = range(lax.axis_size(axis))
    route = [(i - distance, i) for i in devices if i - distance in devices]
    return lax.ppermute(block, axis, route)


def gram_of(left_cols, right_cols):
    return lax.dot_general(
        left_cols,
        right_cols,
        (((0,), (0,)), ((), ())),
        precision=lax.Precision.HIGHEST,
        preferred_element_type=jnp.float32,
    )


def product(left_mat, right_mat):
    return jnp.dot(
        left_mat, right_mat, precision=lax.Precision.HIGHEST, preferred_element_type=jnp.float32
    )


def polar_turn(gram_matrix):
    half_width = gram_matrix.shape[0] // 2
    diagonal = jnp.diagonal(gram_matrix)
    inverse = 1.0 / jnp.sqrt(diagonal + 1e-06)
    cross_part = (
        gram_matrix[:half_width, half_width:]
        * inverse[:half_width, None]
        * inverse[None, half_width:]
    )
    cross_part = cross_part / (1.0 + jnp.sqrt(jnp.sum(cross_part * cross_part)))
    zero_block = jnp.zeros((half_width, half_width), jnp.float32)
    skew_part = jnp.concatenate(
        [
            jnp.concatenate([zero_block, cross_part], 1),
            jnp.concatenate([-cross_part.T, zero_block], 1),
        ],
        0,
    )
    identity = jnp.eye(2 * half_width, dtype=jnp.float32)
    factor = identity + skew_part
    for repeat in range(NEWTON):
        factor = product(factor, 1.5 * identity - 0.5 * gram_of(factor, factor))
    return factor


def pair_rotation(gram_matrix):
    rotation = jnp.eye(gram_matrix.shape[0], dtype=jnp.float32)
    current = gram_matrix
    for sweep_index in range(SWEEPS):
        factor = polar_turn(current)
        rotation = product(rotation, factor)
        if sweep_index + 1 < SWEEPS:
            current = gram_of(factor, product(current, factor))
    return (rotation, current)


def plain_move(upper_block, lower_block):
    pairs_count = lax.axis_size("pair")
    position = lax.axis_index("pair")
    outgoing = jnp.where(position == 0, lower_block, upper_block)
    arrived = shifted(outgoing, "pair", 1)
    below = shifted(lower_block, "pair", -1)
    new_upper = jnp.where(position == 0, upper_block, arrived)
    new_lower = jnp.where(position == pairs_count - 1, upper_block, below)
    return (new_upper, new_lower)


def body(matrix):
    upper_block = matrix[0]
    lower_block = matrix[1]
    half_width = upper_block.shape[1]
    for step_index in range(STEPS):
        pair_cols = jnp.concatenate([upper_block, lower_block], 1)
        gram_matrix = lax.psum(gram_of(pair_cols, pair_cols), "row")
        rotation, current = pair_rotation(gram_matrix)
        rotated = product(pair_cols, rotation)
        upper_block = rotated[:, :half_width]
        lower_block = rotated[:, half_width:]
        upper_block, lower_block = plain_move(upper_block, lower_block)
    return jnp.stack([upper_block, lower_block], 0)


def solution(mesh):
    in_specs = (P(None, "row", "pair"),)
    out_specs = P(None, "row", "pair")
    return jax.shard_map(body, mesh=mesh, in_specs=in_specs, out_specs=out_specs, check_vma=False)
```

profile of v0, /device:TPU:3, one launch (start us, length us, event | category | flops | bytes accessed | tf_op | source)
XLA Modules:
  0.0 806.4 jit_solution(11936363470819997771)
XLA Ops:
  6.5 2.5 slice_bitcast_fusion.1
  9.0 1.3 copy-done.1
  10.4 7.7 fusion.3
  18.5 266.6 %all-reduce.11.cloned.1.call-done = f32[256,256]{1,0:T(8,128)} async-done(((f32[256,256]{1,0:T(8,128)}), f32[256,256]{1,0:T(8,128)}) %all-reduce.11.cloned.1.call-update) | async-done | bytes 262160 | tf_op jit(solution)/shard_map/psum | solution.py:86
  285.1 2.6 gather_fusion
  287.6 1.6 multiply_reduce_fusion.3
  289.9 0.9 negate_bitcast_fusion.3
  295.2 2.9 gather_fusion.1
  298.1 0.7 multiply_reduce_fusion.2
  303.0 4.3 fusion.2
  307.3 2.4 slice_select_fusion.3
  309.8 0.8 copy-done
  310.6 2.2 collective-permute-start
  312.8 4.1 collective-permute-start.1
  316.9 85.5 %collective-permute-done = f32[4096,128]{0,1:T(8,128)S(1)} collective-permute-done((f32[4096,128]{0,1:T(8,128)}, f32[4096,128]{0,1:T(8,128)S(1)}, u32[]{:S(2)}, u32[]{:S(2)}) %collective-permute-start) | collective-permute-done | bytes 2097184 | tf_op jit(solution)/shard_map/ppermute | solution.py:14
  402.4 1.3 copy-done.7
  403.8 2.4 collective-permute-done.1
  406.2 3.3 slice_select_fusion.2
  409.5 1.3 copy-done.3
  410.8 4.2 fusion.1
  415.0 258.3 %all-reduce.13.cloned.1.call-done = f32[256,256]{1,0:T(8,128)} async-done(((f32[256,256]{1,0:T(8,128)}), f32[256,256]{1,0:T(8,128)}) %all-reduce.13.cloned.1.call-update) | async-done | bytes 262160 | tf_op jit(solution)/shard_map/psum | solution.py:86
  673.4 2.6 gather_fusion.2
  675.9 1.6 multiply_reduce_fusion.1
  678.2 0.9 negate_bitcast_fusion.1
  683.5 2.6 gather_fusion.3
  691.0 4.1 fusion
  695.5 2.2 collective-permute-start.2
  697.8 4.0 collective-permute-start.3
  701.7 85.4 %collective-permute-done.2 = f32[4096,128]{0,1:T(8,128)S(1)} collective-permute-done((f32[4096,128]{0,1:T(8,128)S(1)}, f32[4096,128]{0,1:T(8,128)S(1)}, u32[]{:S(2)}, u32[]{:S(2)}) %collective-permute-start.2) | collective-permute-done | bytes 2097184 | tf_op jit(solution)/shard_map/ppermute | solution.py:14
  787.1 3.7 collective-permute-done.3
  791.4 2.4 pad_maximum_fusion.2
  793.8 5.6 copy.15
  (66 shorter events, 17.7 us)
Async XLA Ops:
  6.5 278.5 %all-reduce.11.cloned.1.call-start = ((), (), s32[]{:S(2)}) async-start(), calls=%async_computation | async-start | bytes 524288 | tf_op jit(solution)/shard_map/psum | solution.py:86
  9.0 1.3 copy-start.1
  18.1 655.2 %all-reduce.13.cloned.1.call-start = ((), (), s32[]{:S(2)}) async-start(), calls=%async_computation.1 | async-start | bytes 524288 | tf_op jit(solution)/shard_map/psum | solution.py:86
  291.3 2.9 copy-start.5
  300.6 2.4 copy-start.2
  307.3 3.3 copy-start
  310.6 91.8 %collective-permute-start = (f32[4096,128]{0,1:T(8,128)}, f32[4096,128]{0,1:T(8,128)S(1)}, u32[]{:S(2)}, u32[]{:S(2)}) collective-permute-start(f32[4096,128]{0,1:T(8,128)} %get-tuple-element.19), channel_id=1, source_target_pairs={{0,32},{32,64},{64,96},{96,128},{128,160},{160,192},{192,224},{1,3... | collective-permute-start | bytes 6291464 | tf_op jit(solution)/shard_map/ppermute | solution.py:14
  312.8 93.4 %collective-permute-start.1 = (f32[4096,128]{0,1:T(8,128)}, f32[4096,128]{0,1:T(8,128)}, u32[]{:S(2)}, u32[]{:S(2)}) collective-permute-start(f32[4096,128]{0,1:T(8,128)} %get-tuple-element.20), channel_id=1, source_target_pairs={{32,0},{64,32},{96,64},{128,96},{160,128},{192,160},{224,192},{33,... | collective-permute-start | bytes 6291464 | tf_op jit(solution)/shard_map/ppermute | solution.py:14
  402.4 1.3 copy-start.7
  409.5 1.3 copy-start.3
  679.6 2.9 copy-start.6
  688.6 2.4 copy-start.4
  695.5 91.6 %collective-permute-start.2 = (f32[4096,128]{0,1:T(8,128)S(1)}, f32[4096,128]{0,1:T(8,128)S(1)}, u32[]{:S(2)}, u32[]{:S(2)}) collective-permute-start(f32[4096,128]{0,1:T(8,128)S(1)} %get-tuple-element.15), channel_id=1, source_target_pairs={{0,32},{32,64},{64,96},{96,128},{128,160},{160,192},{192,224},{1,3... | collective-permute-start | bytes 6291464 | tf_op jit(solution)/shard_map/ppermute | solution.py:14
  697.8 93.1 %collective-permute-start.3 = (f32[4096,128]{0,1:T(8,128)S(1)}, f32[4096,128]{0,1:T(8,128)S(1)}, u32[]{:S(2)}, u32[]{:S(2)}) collective-permute-start(f32[4096,128]{0,1:T(8,128)S(1)} %get-tuple-element.16), channel_id=1, source_target_pairs={{32,0},{64,32},{96,64},{128,96},{160,128},{192,160},{224,192},{33,... | collective-permute-start | bytes 6291464 | tf_op jit(solution)/shard_map/ppermute | solution.py:14
Sparse Core Ops, SparseCore 0:
  18.2 266.7 all-reduce.10
  415.2 258.1 all-reduce.12
where the time goes:
time: 812 us; the launch traced here: 806 us
  waiting for transfers between devices  702 us (86%)
  matrix products  35.4 us (4%)
  local copies, waits for them, and re-layouts  23.8 us (3%)
  between operations  16.7 us (2%)
  other arithmetic  15.7 us (2%)
  starting transfers between devices  12.9 us (2%)
    psum x2, waiting for transfers between devices, body(): gram_matrix = lax.psum(gram_of(pair_cols, pair_cols), 'row')  525 us
    ppermute x4, waiting for transfers between devices, shifted(): return lax.ppermute(block, axis, route)  177 us
    dot_general x16, matrix products, gram_of(): lax.dot_general(left_cols, right_cols, (((0,), (0,)), ((), ())), precisio...  19.7 us
  transfers between devices with their start and end apart: 6, of which 6 were waited for; matrix products, arithmetic and copies ran while one was open for 0% of the time, Pallas kernels for 0%

commit v1 on v0

--- a/solution.py
+++ b/solution.py
@@ -83,7 +83,7 @@
     half_width = upper_block.shape[1]
     for step_index in range(STEPS):
         pair_cols = jnp.concatenate([upper_block, lower_block], 1)
-        gram_matrix = lax.psum(gram_of(pair_cols, pair_cols), "row")
+        gram_matrix = jnp.sum(lax.all_gather(gram_of(pair_cols, pair_cols), "row"), axis=0)
         rotation, current = pair_rotation(gram_matrix)
         rotated = product(pair_cols, rotation)
         upper_block = rotated[:, :half_width]

time: 812 us -> 495 us (0.61)
  waiting for transfers between devices: 702 us -> 380 us
    psum x2 -> x0, waiting for transfers between devices: 525 us -> none  [body(): gram_matrix = lax.psum(gram_of(pair_cols, pair_cols), 'row')]
    all_gather x0 -> x2, waiting for transfers between devices: none -> 203 us  [body(): lax.all_gather(gram_of(pair_cols, pair_cols), 'row')]
where the time goes in v1:
time: 495 us; the launch traced here: 489 us
  waiting for transfers between devices  380 us (77%)
  matrix products  35.5 us (7%)
  local copies, waits for them, and re-layouts  23.4 us (5%)
  other arithmetic  20.4 us (4%)
  between operations  16.9 us (3%)
  starting transfers between devices  12.9 us (3%)
    all_gather x2, waiting for transfers between devices, body(): lax.all_gather(gram_of(pair_cols, pair_cols), 'row')  203 us
    ppermute x4, waiting for transfers between devices, shifted(): return lax.ppermute(block, axis, route)  177 us
    dot_general x16, matrix products, gram_of(): lax.dot_general(left_cols, right_cols, (((0,), (0,)), ((), ())), precisio...  19.7 us
    dot_general x20, matrix products, product(): jnp.dot(left_mat, right_mat, precision=lax.Precision.HIGHEST, preferred_e...  15.8 us
    ppermute x4, starting transfers between devices, shifted(): return lax.ppermute(block, axis, route)  12.5 us
    gather x4, local copies, waits for them, and re-layouts, polar_turn(): diagonal = jnp.diagonal(gram_matrix)  10.1 us
  transfers between devices with their start and end apart: 6, of which 6 were waited for; matrix products, arithmetic and copies ran while one was open for 0% of the time, Pallas kernels for 0%

profile of v1, /device:TPU:3, one launch (start us, length us, event | category | flops | bytes accessed | tf_op | source)
XLA Modules:
  0.0 489.2 jit_solution(6267648469510312191)
XLA Ops:
  6.5 2.5 slice_bitcast_fusion.1
  9.0 1.3 copy-done.1
  10.4 7.8 %fusion.3 = f32[256,256]{1,0:T(8,128)} fusion(f32[4096,128]{1,0:T(8,128)S(1)} %get-tuple-element.22, f32[4096,128]{1,0:T(8,128)S(1)} %get-tuple-element.21), kind=kOutput, calls=%fused_computation.10 | convolution fusion | flops 3222274048 | bytes 4456448 | tf_op jit(solution)/shard_map/dot_general | solution.py:18
  18.5 104.6 %all-gather.5.cloned.1.call-done = f32[8192,256]{1,0:T(8,128)} async-done(((f32[256,256]{1,0:T(8,128)}), f32[8192,256]{1,0:T(8,128)}) %all-gather.5.cloned.1.call-update) | async-done | bytes 8388624 | tf_op jit(solution)/shard_map/all_gather | solution.py:86
  123.1 3.9 reduce_sum.54
  127.1 2.3 gather_fusion
  129.4 0.8 multiply_reduce_fusion.3
  135.3 2.9 gather_fusion.1
  138.2 0.8 multiply_reduce_fusion.2
  143.2 4.3 fusion.2
  147.5 2.4 slice_select_fusion.3
  150.0 0.8 copy-done
  150.8 2.2 collective-permute-start
  153.0 4.1 collective-permute-start.1
  157.2 85.9 %collective-permute-done = f32[4096,128]{0,1:T(8,128)S(1)} collective-permute-done((f32[4096,128]{0,1:T(8,128)}, f32[4096,128]{0,1:T(8,128)S(1)}, u32[]{:S(2)}, u32[]{:S(2)}) %collective-permute-start) | collective-permute-done | bytes 2097184 | tf_op jit(solution)/shard_map/ppermute | solution.py:14
  243.0 1.3 copy-done.5
  244.3 2.1 collective-permute-done.1
  246.4 3.3 slice_select_fusion.2
  249.7 1.3 copy-done.3
  251.0 4.3 fusion.1
  255.3 98.6 %all-gather.7.cloned.1.call-done = f32[8192,256]{1,0:T(8,128)} async-done(((f32[256,256]{1,0:T(8,128)}), f32[8192,256]{1,0:T(8,128)}) %all-gather.7.cloned.1.call-update) | async-done | bytes 8388624 | tf_op jit(solution)/shard_map/all_gather | solution.py:86
  353.9 3.9 reduce_sum.57
  357.9 2.3 gather_fusion.2
  360.2 0.8 multiply_reduce_fusion.1
  366.1 2.6 gather_fusion.3
  373.7 4.1 fusion
  378.3 2.2 collective-permute-start.2
  380.5 4.0 collective-permute-start.3
  384.5 85.7 %collective-permute-done.2 = f32[4096,128]{0,1:T(8,128)S(1)} collective-permute-done((f32[4096,128]{0,1:T(8,128)S(1)}, f32[4096,128]{0,1:T(8,128)S(1)}, u32[]{:S(2)}, u32[]{:S(2)}) %collective-permute-start.2) | collective-permute-done | bytes 2097184 | tf_op jit(solution)/shard_map/ppermute | solution.py:14
  470.2 3.4 collective-permute-done.3
  474.1 2.4 pad_maximum_fusion.2
  476.5 5.6 %copy.15 = f32[2,4096,128]{2,1,0:T(8,128)} copy(f32[2,4096,128]{1,2,0:T(8,128)} %pad_maximum_fusion.2) | data formatting | bytes 8388608 | tf_op jit(solution)/shard_map/stack | solution.py:92
  (64 shorter events, 17.9 us)
Async XLA Ops:
  6.5 116.6 %all-gather.5.cloned.1.call-start = ((), (), s32[]{:S(2)}) async-start(), calls=%async_computation | async-start | bytes 8650752 | tf_op jit(solution)/shard_map/all_gather | solution.py:86
  9.0 1.3 copy-start.1
  18.1 335.8 %all-gather.7.cloned.1.call-start = ((), (), s32[]{:S(2)}) async-start(), calls=%async_computation.1 | async-start | bytes 8650752 | tf_op jit(solution)/shard_map/all_gather | solution.py:86
  140.8 2.4 copy-start.2
  147.5 3.3 copy-start
  150.8 92.2 %collective-permute-start = (f32[4096,128]{0,1:T(8,128)}, f32[4096,128]{0,1:T(8,128)S(1)}, u32[]{:S(2)}, u32[]{:S(2)}) collective-permute-start(f32[4096,128]{0,1:T(8,128)} %get-tuple-element.19), channel_id=1, source_target_pairs={{0,32},{32,64},{64,96},{96,128},{128,160},{160,192},{192,224},{1,3... | collective-permute-start | bytes 6291464 | tf_op jit(solution)/shard_map/ppermute | solution.py:14
  153.0 93.4 %collective-permute-start.1 = (f32[4096,128]{0,1:T(8,128)}, f32[4096,128]{0,1:T(8,128)}, u32[]{:S(2)}, u32[]{:S(2)}) collective-permute-start(f32[4096,128]{0,1:T(8,128)} %get-tuple-element.20), channel_id=1, source_target_pairs={{32,0},{64,32},{96,64},{128,96},{160,128},{192,160},{224,192},{33,... | collective-permute-start | bytes 6291464 | tf_op jit(solution)/shard_map/ppermute | solution.py:14
  243.0 1.3 copy-start.5
  249.7 1.3 copy-start.3
  371.3 2.4 copy-start.4
  378.3 91.9 %collective-permute-start.2 = (f32[4096,128]{0,1:T(8,128)S(1)}, f32[4096,128]{0,1:T(8,128)S(1)}, u32[]{:S(2)}, u32[]{:S(2)}) collective-permute-start(f32[4096,128]{0,1:T(8,128)S(1)} %get-tuple-element.15), channel_id=1, source_target_pairs={{0,32},{32,64},{64,96},{96,128},{128,160},{160,192},{192,224},{1,3... | collective-permute-start | bytes 6291464 | tf_op jit(solution)/shard_map/ppermute | solution.py:14
  380.5 93.1 %collective-permute-start.3 = (f32[4096,128]{0,1:T(8,128)S(1)}, f32[4096,128]{0,1:T(8,128)S(1)}, u32[]{:S(2)}, u32[]{:S(2)}) collective-permute-start(f32[4096,128]{0,1:T(8,128)S(1)} %get-tuple-element.16), channel_id=1, source_target_pairs={{32,0},{64,32},{96,64},{128,96},{160,128},{192,160},{224,192},{33,... | collective-permute-start | bytes 6291464 | tf_op jit(solution)/shard_map/ppermute | solution.py:14
Sparse Core Ops, SparseCore 0:
  18.3 104.7 all-gather.4
  255.4 98.4 all-gather.6
